TPU v7x, 32 devices: a whole 2x2x4 slice. The times are simulated.
32 devices in a mesh: groups: 2 (over y), hosts: 4 (over z), mp: 4 (over x, core).
Axes of the slice: x: 2, y: 2, z: 4, core: 2. Of those that a mesh axis runs over, the one named last changes fastest.
Arguments:
- hidden: bfloat16 [256, 4096], P(('groups', 'hosts'), 'mp'), parts along dimension 0, may hold values from -6 to 6
- base_query_projection: bfloat16 [256, 4096], P(('groups', 'hosts'), 'mp'), parts along dimension 0, may hold values from -160 to 160
- base_key_projection: bfloat16 [256, 4096], P(('groups', 'hosts'), 'mp'), parts along dimension 0, may hold values from -6 to 6
- base_value_projection: bfloat16 [256, 4096], P(('groups', 'hosts'), 'mp'), parts along dimension 0, may hold values from -6 to 6
- adapter_input_factors: bfloat16 [8, 4096, 128], P(('groups', 'hosts'), 'mp'), parts along dimension 0, may hold values from -0.09375 to 0.09375
- adapter_output_factors: bfloat16 [8, 2, 64, 4096], P(('groups', 'hosts'), None, None, 'mp'), parts along dimension 0, may hold values from -0.75 to 0.75
- statement_prefix_cache: bfloat16 [32, 2, 128, 4096], P(('groups', 'hosts'), None, None, 'mp'), parts along dimension 0, may hold values from -6 to 6
- generated_token_cache: bfloat16 [256, 2, 8, 4096], P(('groups', 'hosts'), None, None, 'mp'), parts along dimension 0, may hold values from -6 to 6
- attempt_theorem_index: int32 [256], P(('groups', 'hosts')), parts along dimension 0, may hold values from 0 to 3, as said below
- host_live_count: int32 [8], P(('groups', 'hosts')), parts along dimension 0, may hold values from 8 to 32, as said below
- adapter_pool_row: int32 [8], P('groups'), parts along dimension 0, may hold values from 0 to 3, as said below
- prefix_pool_row: int32 [8, 4], P('groups'), parts along dimension 0, may hold values from 0 to 15, as said below
- prefix_block_count: int32 [8], P('groups'), parts along dimension 0, may hold values from 1 to 4
Outputs:
- attended: bfloat16 [256, 4096], P(('groups', 'hosts'), 'mp'), parts along dimension 0
- key_rows: bfloat16 [256, 4096], P(('groups', 'hosts'), 'mp'), parts along dimension 0
- value_rows: bfloat16 [256, 4096], P(('groups', 'hosts'), 'mp'), parts along dimension 0
There are 2 independent parts, one for each index of `groups`. A program takes and returns all parts, laid end to end along the dimension named above; each array names one. Nothing has to cross between parts.
Inputs may be any that keep to these rules, and one draw needn't show every extreme that they name: `attempt_theorem_index`: among the live attempts of one host, at most 8 name theorems whose adapter lies on any one host, and for each block index at most 8 name theorems whose block of that index lies on any one host. One host holds the adapters named by 8 live attempts of every host, and one host holds the first blocks named by 8 live attempts of every host. `host_live_count`: rows at or above a host's count are empty; some host has all 32 rows live. `adapter_pool_row`: all entries differ; pool row p lies on host p. `prefix_pool_row`: all entries differ; pool row p lies on host p // 4.
All inputs are finite; a program needn't handle non-finite values.
Results may differ from a plain program's by a relative error of at most 0.011.
Values may be sent and summed in bfloat16 or wider, within the bound.
No kernel may reach another device: no remote copies, remote signals or barrier semaphores. Data moves between devices by JAX's collectives and lax.ppermute only.
A program may use at most 64 MiB of HBM per device.

v0:
```python
import jax
import jax.numpy as jnp
from jax import lax
from jax.sharding import PartitionSpec as P

HEAD_SIZE = 128
ADAPTER_RANK = 64
BLK = 128
PBLK = 4
ADAPTER_SCALE = 0.5
ROPE_BASE = 10000.0
NEG_FILL = -1e30


def rotate(values, position):
    shaped = values.reshape(values.shape[:-1] + (-1, HEAD_SIZE))
    halfway = HEAD_SIZE // 2
    frequency = ROPE_BASE ** (-(jnp.arange(halfway, dtype=jnp.float32) * (2.0 / HEAD_SIZE)))
    angles = position.astype(jnp.float32)[..., None] * frequency
    cosine = jnp.cos(angles)[..., None, :]
    sine_part = jnp.sin(angles)[..., None, :]
    first_half = shaped[..., :halfway]
    second = shaped[..., halfway:]
    turned = jnp.concatenate(
        [first_half * cosine - second * sine_part, second * cosine + first_half * sine_part],
        axis=-1,
    )
    return turned.reshape(values.shape)


def lookup_table(source_table, wanted):
    matches = wanted[:, None] == jnp.arange(source_table.shape[0], dtype=jnp.int32)[None, :]
    if source_table.ndim == 1:
        return jnp.sum(jnp.where(matches, source_table[None, :], 0), axis=1)
    return jnp.sum(jnp.where(matches[:, :, None], source_table[None, :, :], 0), axis=1)


def route_matrix(destination, validity, capacity, host_total):
    ordinal = jnp.arange(destination.shape[0], dtype=jnp.int32)
    earlier = (
        (destination[:, None] == destination[None, :])
        & validity[None, :]
        & (ordinal[None, :] < ordinal[:, None])
    )
    ranking = jnp.sum(earlier.astype(jnp.int32), axis=1)
    target = destination * capacity + ranking
    places = jnp.arange(host_total * capacity, dtype=jnp.int32)
    return ((places[:, None] == target[None, :]) & validity[None, :]).astype(jnp.bfloat16)


def pack_rows(router, payload):
    return jnp.dot(router, payload, preferred_element_type=jnp.float32).astype(jnp.bfloat16)


def attend_local(queries, chosen, statement_prefix_cache):
    head_count = queries.shape[-1] // HEAD_SIZE
    blocks = statement_prefix_cache.shape[0]
    block_keys = statement_prefix_cache[:, 0].reshape(
        blocks, statement_prefix_cache.shape[2], head_count, HEAD_SIZE
    )
    block_values = statement_prefix_cache[:, 1].reshape(
        blocks, statement_prefix_cache.shape[2], head_count, HEAD_SIZE
    )
    shaped = queries.reshape(queries.shape[:-1] + (head_count, HEAD_SIZE))
    scores = jnp.einsum(
        "nchd,bthd->ncbht", shaped, block_keys, preferred_element_type=jnp.float32
    ) * HEAD_SIZE ** (-0.5)
    chosen_mask = (chosen > 0)[:, :, :, None, None]
    masked = jnp.where(chosen_mask, scores, NEG_FILL)
    top_score = jnp.max(masked, axis=(2, 4))
    weights = jnp.where(chosen_mask, jnp.exp(masked - top_score[:, :, None, :, None]), 0.0)
    totals = jnp.sum(weights, axis=(2, 4))
    mixed_rows = jnp.einsum(
        "ncbht,bthd->nchd",
        weights.astype(jnp.bfloat16),
        block_values,
        preferred_element_type=jnp.float32,
    )
    return (mixed_rows.reshape(queries.shape), top_score, totals)


def body(
    hidden,
    base_query_projection,
    base_key_projection,
    base_value_projection,
    adapter_input_factors,
    adapter_output_factors,
    statement_prefix_cache,
    generated_token_cache,
    attempt_theorem_index,
    host_live_count,
    adapter_pool_row,
    prefix_pool_row,
    prefix_block_count,
):
    host_total = lax.axis_size("hosts")
    attempts = hidden.shape[0]
    capacity = max(1, attempts // host_total)
    owner_held_rows = adapter_input_factors.shape[0]
    local_blocks = statement_prefix_cache.shape[0]
    row_width = base_query_projection.shape[1]
    head_count = row_width // HEAD_SIZE
    ordinal = jnp.arange(attempts, dtype=jnp.int32)
    living = ordinal < host_live_count[0]
    adapter_rows = lookup_table(adapter_pool_row, attempt_theorem_index)
    block_rows = lookup_table(prefix_pool_row, attempt_theorem_index)
    block_counts = lookup_table(prefix_block_count, attempt_theorem_index)
    position = BLK * block_counts + generated_token_cache.shape[2]
    adapter_router = route_matrix(adapter_rows // owner_held_rows, living, capacity, host_total)
    adapter_pick = (
        adapter_rows[:, None] % owner_held_rows
        == jnp.arange(owner_held_rows, dtype=jnp.int32)[None, :]
    ).astype(jnp.bfloat16)
    sent_hidden = pack_rows(adapter_router, hidden).reshape(host_total, capacity, hidden.shape[1])
    sent_pick = pack_rows(adapter_router, adapter_pick).reshape(
        host_total, capacity, owner_held_rows
    )
    incoming_rows = lax.all_to_all(sent_hidden, "hosts", split_axis=0, concat_axis=0, tiled=True)
    pick_in = lax.all_to_all(sent_pick, "hosts", split_axis=0, concat_axis=0, tiled=True)
    projected_rows = jnp.einsum(
        "xjp,epk->xjek", incoming_rows, adapter_input_factors, preferred_element_type=jnp.float32
    )
    partial_rank = jnp.sum(projected_rows * pick_in.astype(jnp.float32)[..., None], axis=2)
    rank_rows = lax.psum(partial_rank, "mp").astype(jnp.bfloat16)
    spread_rows = rank_rows[:, :, None, :] * pick_in[..., None]
    query_correction = jnp.einsum(
        "exqw,qwf->exf",
        spread_rows[..., :ADAPTER_RANK],
        adapter_output_factors[:, 0],
        preferred_element_type=jnp.float32,
    )
    value_correction = jnp.einsum(
        "exqw,qwf->exf",
        spread_rows[..., ADAPTER_RANK:],
        adapter_output_factors[:, 1],
        preferred_element_type=jnp.float32,
    )
    adapter_corrections = (
        jnp.concatenate([query_correction, value_correction], axis=-1) * ADAPTER_SCALE
    ).astype(jnp.bfloat16)
    returned = lax.all_to_all(adapter_corrections, "hosts", split_axis=0, concat_axis=0, tiled=True)
    adapter_corrections = jnp.dot(
        adapter_router.T,
        returned.reshape(host_total * capacity, 2 * row_width),
        preferred_element_type=jnp.float32,
    )
    query_rows = rotate(
        base_query_projection.astype(jnp.float32) + adapter_corrections[:, :row_width], position
    ).astype(jnp.bfloat16)
    value_rows = (
        base_value_projection.astype(jnp.float32) + adapter_corrections[:, row_width:]
    ).astype(jnp.bfloat16)
    key_rows = rotate(base_key_projection.astype(jnp.float32), position).astype(jnp.bfloat16)
    requests = []
    for block_index in range(PBLK):
        wanted = living & (block_index < block_counts)
        holder = block_rows[:, block_index]
        router = route_matrix(holder // local_blocks, wanted, capacity, host_total)
        block_pick = (
            holder[:, None] % local_blocks == jnp.arange(local_blocks, dtype=jnp.int32)[None, :]
        ).astype(jnp.bfloat16)
        sent_queries = pack_rows(router, query_rows).reshape(host_total, capacity, row_width)
        sent_blocks = pack_rows(router, block_pick).reshape(host_total, capacity, local_blocks)
        requests.append((router, wanted, sent_queries, sent_blocks))
    partials = []
    for request in requests:
        answer_mixed_rows, answer_top_score, answer_totals = attend_local(
            lax.all_to_all(request[2], "hosts", split_axis=0, concat_axis=0, tiled=True),
            lax.all_to_all(request[3], "hosts", split_axis=0, concat_axis=0, tiled=True),
            statement_prefix_cache,
        )
        partials.append(
            (
                lax.all_to_all(answer_mixed_rows, "hosts", split_axis=0, concat_axis=0, tiled=True),
                lax.all_to_all(answer_top_score, "hosts", split_axis=0, concat_axis=0, tiled=True),
                lax.all_to_all(answer_totals, "hosts", split_axis=0, concat_axis=0, tiled=True),
            )
        )
    entries = []
    for block_index in range(PBLK):
        router, wanted = (requests[block_index][0], requests[block_index][1])
        mixed_rows, top_score, totals = partials[block_index]
        back_router = router.T.astype(jnp.float32)
        flat_mixed = jnp.dot(
            back_router,
            mixed_rows.reshape(host_total * capacity, row_width),
            precision=lax.Precision.HIGHEST,
        )
        flat_top = jnp.dot(
            back_router,
            top_score.reshape(host_total * capacity, head_count),
            precision=lax.Precision.HIGHEST,
        )
        flat_totals = jnp.dot(
            back_router,
            totals.reshape(host_total * capacity, head_count),
            precision=lax.Precision.HIGHEST,
        )
        flat_top = jnp.where(wanted[:, None], flat_top, NEG_FILL)
        entries.append((flat_mixed, flat_top, flat_totals))
    shaped_query = query_rows.reshape(attempts, head_count, HEAD_SIZE)
    own_keys = jnp.concatenate([generated_token_cache[:, 0], key_rows[:, None, :]], axis=1).reshape(
        attempts, -1, head_count, HEAD_SIZE
    )
    own_values = jnp.concatenate(
        [generated_token_cache[:, 1], value_rows[:, None, :]], axis=1
    ).reshape(attempts, -1, head_count, HEAD_SIZE)
    own_scores = jnp.einsum(
        "ahd,athd->aht", shaped_query, own_keys, preferred_element_type=jnp.float32
    ) * HEAD_SIZE ** (-0.5)
    own_top = jnp.max(own_scores, axis=2)
    own_weights = jnp.exp(own_scores - own_top[..., None])
    own_totals = jnp.sum(own_weights, axis=2)
    own_mixed = jnp.einsum(
        "aht,athd->ahd",
        own_weights.astype(jnp.bfloat16),
        own_values,
        preferred_element_type=jnp.float32,
    )
    overall = own_top
    for flat_mixed, flat_top, flat_totals in entries:
        overall = jnp.maximum(overall, flat_top)
    own_factor = jnp.exp(own_top - overall)
    numerator = own_mixed * own_factor[..., None]
    denominator = own_totals * own_factor
    for flat_mixed, flat_top, flat_totals in entries:
        factor = jnp.exp(flat_top - overall)
        numerator = (
            numerator + flat_mixed.reshape(attempts, head_count, HEAD_SIZE) * factor[..., None]
        )
        denominator = denominator + flat_totals * factor
    attended = (numerator / denominator[..., None]).reshape(attempts, row_width)
    live_rows = living[:, None]
    return (
        jnp.where(live_rows, attended, 0.0).astype(jnp.bfloat16),
        jnp.where(live_rows, key_rows, 0.0),
        jnp.where(live_rows, value_rows, 0.0),
    )


def solution(mesh):
    placed = (
        P(("groups", "hosts"), "mp"),
        P(("groups", "hosts"), "mp"),
        P(("groups", "hosts"), "mp"),
        P(("groups", "hosts"), "mp"),
        P(("groups", "hosts"), "mp", None),
        P(("groups", "hosts"), None, None, "mp"),
        P(("groups", "hosts"), None, None, "mp"),
        P(("groups", "hosts"), None, None, "mp"),
        P(("groups", "hosts")),
        P(("groups", "hosts")),
        P("groups"),
        P("groups", None),
        P("groups"),
    )
    return jax.shard_map(
        body,
        mesh=mesh,
        in_specs=placed,
        out_specs=(
            P(("groups", "hosts"), "mp"),
            P(("groups", "hosts"), "mp"),
            P(("groups", "hosts"), "mp"),
        ),
        check_vma=False,
    )
```

profile of v0, /device:TPU:0, one launch (start us, length us, event | category | flops | bytes accessed | tf_op | source)
XLA Modules:
  0.0 238.8 jit_solution(13844421475531033518)
XLA Ops:
  3.2 6.3 %all-to-all-start.1 = ((bf16[4,8,1]{1,2,0:T(2,128)(2,1)}), bf16[4,8,1]{1,2,0:T(2,128)(2,1)S(1)}, u32[]{:S(2)}, u32[]{:S(2)}) async-start(bf16[4,8,1]{1,2,0:T(2,128)(2,1)} %reshape.598), calls=%async_computation.1 | async-start | bytes 4096 | tf_op jit(solution)/shard_map/all_to_all | solution.py:120
  23.4 5.1 %all-to-all-start.3 = ((bf16[4,8,4]{1,2,0:T(4,128)(2,1)}), bf16[4,8,4]{1,2,0:T(4,128)(2,1)S(1)}, u32[]{:S(2)}, u32[]{:S(2)}) async-start(bf16[4,8,4]{1,2,0:T(4,128)(2,1)} %copy.229), calls=%async_computation.3 | async-start | bytes 8192 | tf_op jit(solution)/shard_map/all_to_all | solution.py:170
  28.5 5.6 %all-to-all-done.3 = bf16[4,8,4]{1,2,0:T(4,128)(2,1)S(1)} async-done(((bf16[4,8,4]{1,2,0:T(4,128)(2,1)}), bf16[4,8,4]{1,2,0:T(4,128)(2,1)S(1)}, u32[]{:S(2)}, u32[]{:S(2)}) %all-to-all-start.3) | async-done | bytes 288 | tf_op jit(solution)/shard_map/all_to_all | solution.py:170
  37.9 4.8 %all-to-all-done.6 = bf16[4,8,4]{1,2,0:T(4,128)(2,1)S(1)} async-done(((bf16[4,8,4]{1,2,0:T(4,128)(2,1)}), bf16[4,8,4]{1,2,0:T(4,128)(2,1)S(1)}, u32[]{:S(2)}, u32[]{:S(2)}) %all-to-all-start.6) | async-done | bytes 288 | tf_op jit(solution)/shard_map/all_to_all | solution.py:170
  46.6 4.9 %all-to-all-done.9 = bf16[4,8,4]{1,2,0:T(4,128)(2,1)S(1)} async-done(((bf16[4,8,4]{1,2,0:T(4,128)(2,1)}), bf16[4,8,4]{1,2,0:T(4,128)(2,1)S(1)}, u32[]{:S(2)}, u32[]{:S(2)}) %all-to-all-start.9) | async-done | bytes 288 | tf_op jit(solution)/shard_map/all_to_all | solution.py:170
  55.4 5.1 %all-to-all-done = bf16[4,8,1024]{2,1,0:T(8,128)(2,1)S(1)} async-done(((bf16[4,8,1024]{2,1,0:T(8,128)(2,1)}), bf16[4,8,1024]{2,1,0:T(8,128)(2,1)S(1)}, u32[]{:S(2)}, u32[]{:S(2)}) %all-to-all-start) | async-done | bytes 65568 | tf_op jit(solution)/shard_map/all_to_all | solution.py:119
  63.9 10.4 %psum.7 = bf16[4,8,128]{2,1,0:T(8,128)(2,1)S(1)} all-reduce(f32[4,8,128]{2,1,0:T(8,128)S(1)} %convolution_multiply_fusion.8), channel_id=1, replica_groups=mesh['groups'=2,'hosts'=4,'mp'=4] {'mp'}, use_global_device_ids=true, to_apply=%region_2.3 | all-reduce | flops 4096 | bytes 24576 | tf_op jit(solution)/shard_map/psum | solution.py:125
  77.2 4.8 %all-to-all-start.2 = ((bf16[4,8,2048]{2,1,0:T(8,128)(2,1)}), bf16[4,8,2048]{2,1,0:T(8,128)(2,1)S(1)}, u32[]{:S(2)}, u32[]{:S(2)}) async-start(bf16[4,8,2048]{2,1,0:T(8,128)(2,1)} %fusion.52), calls=%async_computation.2 | async-start | bytes 262144 | tf_op jit(solution)/shard_map/all_to_all | solution.py:142
  82.6 5.3 %all-to-all-done.2 = bf16[4,8,2048]{2,1,0:T(8,128)(2,1)S(1)} async-done(((bf16[4,8,2048]{2,1,0:T(8,128)(2,1)}), bf16[4,8,2048]{2,1,0:T(8,128)(2,1)S(1)}, u32[]{:S(2)}, u32[]{:S(2)}) %all-to-all-start.2) | async-done | bytes 131104 | tf_op jit(solution)/shard_map/all_to_all | solution.py:142
  99.1 5.0 %all-to-all-start.10 = ((bf16[4,8,1024]{2,1,0:T(8,128)(2,1)}), bf16[4,8,1024]{2,1,0:T(8,128)(2,1)S(1)}, u32[]{:S(2)}, u32[]{:S(2)}) async-start(bf16[4,8,1024]{2,1,0:T(8,128)(2,1)} %fusion.17), calls=%async_computation.10 | async-start | bytes 131072 | tf_op jit(solution)/shard_map/all_to_all | solution.py:169
  105.1 4.8 %all-to-all-done.10 = bf16[4,8,1024]{2,1,0:T(8,128)(2,1)S(1)} async-done(((bf16[4,8,1024]{2,1,0:T(8,128)(2,1)}), bf16[4,8,1024]{2,1,0:T(8,128)(2,1)S(1)}, u32[]{:S(2)}, u32[]{:S(2)}) %all-to-all-start.10) | async-done | bytes 65568 | tf_op jit(solution)/shard_map/all_to_all | solution.py:169
  114.2 4.7 %all-to-all-done.7 = bf16[4,8,1024]{2,1,0:T(8,128)(2,1)S(1)} async-done(((bf16[4,8,1024]{2,1,0:T(8,128)(2,1)}), bf16[4,8,1024]{2,1,0:T(8,128)(2,1)S(1)}, u32[]{:S(2)}, u32[]{:S(2)}) %all-to-all-start.7) | async-done | bytes 65568 | tf_op jit(solution)/shard_map/all_to_all | solution.py:169
  127.9 4.3 %all-to-all-start.20 = ((f32[4,8,8]{1,2,0:T(8,128)}), f32[4,8,8]{1,2,0:T(8,128)S(1)}, u32[]{:S(2)}, u32[]{:S(2)}) async-start(f32[4,8,8]{1,2,0:T(8,128)} %copy.265), calls=%async_computation.20 | async-start | bytes 32768 | tf_op jit(solution)/shard_map/all_to_all | solution.py:177
  142.7 4.0 %all-to-all-done.8 = f32[4,8,8]{1,2,0:T(8,128)S(1)} async-done(((f32[4,8,8]{1,2,0:T(8,128)}), f32[4,8,8]{1,2,0:T(8,128)S(1)}, u32[]{:S(2)}, u32[]{:S(2)}) %all-to-all-start.8) | async-done | bytes 1056 | tf_op jit(solution)/shard_map/all_to_all | solution.py:176
  151.7 3.9 %all-to-all-done.21 = f32[4,8,8]{1,2,0:T(8,128)S(1)} async-done(((f32[4,8,8]{1,2,0:T(8,128)}), f32[4,8,8]{1,2,0:T(8,128)S(1)}, u32[]{:S(2)}, u32[]{:S(2)}) %all-to-all-start.21) | async-done | bytes 1056 | tf_op jit(solution)/shard_map/all_to_all | solution.py:177
  160.4 4.0 %all-to-all-done.11 = f32[4,8,8]{1,2,0:T(8,128)S(1)} async-done(((f32[4,8,8]{1,2,0:T(8,128)}), f32[4,8,8]{1,2,0:T(8,128)S(1)}, u32[]{:S(2)}, u32[]{:S(2)}) %all-to-all-start.11) | async-done | bytes 1056 | tf_op jit(solution)/shard_map/all_to_all | solution.py:176
  169.4 3.8 %all-to-all-done.22 = f32[4,8,8]{1,2,0:T(8,128)S(1)} async-done(((f32[4,8,8]{1,2,0:T(8,128)}), f32[4,8,8]{1,2,0:T(8,128)S(1)}, u32[]{:S(2)}, u32[]{:S(2)}) %all-to-all-start.22) | async-done | bytes 1056 | tf_op jit(solution)/shard_map/all_to_all | solution.py:177
  182.0 3.7 %all-to-all-start.19 = ((f32[4,8,8]{1,2,0:T(8,128)}), f32[4,8,8]{1,2,0:T(8,128)S(1)}, u32[]{:S(2)}, u32[]{:S(2)}) async-start(f32[4,8,8]{1,2,0:T(8,128)} %copy.263), calls=%async_computation.19 | async-start | bytes 32768 | tf_op jit(solution)/shard_map/all_to_all | solution.py:177
  186.1 5.3 %all-to-all-done.19 = f32[4,8,8]{1,2,0:T(8,128)S(1)} async-done(((f32[4,8,8]{1,2,0:T(8,128)}), f32[4,8,8]{1,2,0:T(8,128)S(1)}, u32[]{:S(2)}, u32[]{:S(2)}) %all-to-all-start.19) | async-done | bytes 1056 | tf_op jit(solution)/shard_map/all_to_all | solution.py:177
  195.3 4.9 %all-to-all-done.5 = f32[4,8,8]{1,2,0:T(8,128)S(1)} async-done(((f32[4,8,8]{1,2,0:T(8,128)}), f32[4,8,8]{1,2,0:T(8,128)S(1)}, u32[]{:S(2)}, u32[]{:S(2)}) %all-to-all-start.5) | async-done | bytes 1056 | tf_op jit(solution)/shard_map/all_to_all | solution.py:176
  204.9 4.5 %all-to-all-done.16 = f32[4,8,1024]{2,1,0:T(8,128)S(1)} async-done(((f32[4,8,1024]{2,1,0:T(8,128)}), f32[4,8,1024]{2,1,0:T(8,128)S(1)}, u32[]{:S(2)}, u32[]{:S(2)}) %all-to-all-start.16) | async-done | bytes 131104 | tf_op jit(solution)/shard_map/all_to_all | solution.py:175
  213.0 6.0 %all-to-all-done.17 = f32[4,8,1024]{2,1,0:T(8,128)S(1)} async-done(((f32[4,8,1024]{2,1,0:T(8,128)}), f32[4,8,1024]{2,1,0:T(8,128)S(1)}, u32[]{:S(2)}, u32[]{:S(2)}) %all-to-all-start.17) | async-done | bytes 131104 | tf_op jit(solution)/shard_map/all_to_all | solution.py:175
  222.9 5.7 %all-to-all-done.18 = f32[4,8,1024]{2,1,0:T(8,128)S(1)} async-done(((f32[4,8,1024]{2,1,0:T(8,128)}), f32[4,8,1024]{2,1,0:T(8,128)S(1)}, u32[]{:S(2)}, u32[]{:S(2)}) %all-to-all-start.18) | async-done | bytes 131104 | tf_op jit(solution)/shard_map/all_to_all | solution.py:175
  232.1 5.6 %all-to-all-done.15 = f32[4,8,1024]{2,1,0:T(8,128)S(1)} async-done(((f32[4,8,1024]{2,1,0:T(8,128)}), f32[4,8,1024]{2,1,0:T(8,128)S(1)}, u32[]{:S(2)}, u32[]{:S(2)}) %all-to-all-start.15) | async-done | bytes 131104 | tf_op jit(solution)/shard_map/all_to_all | solution.py:175
  (238 shorter events, 113.7 us)
Async XLA Ops:
  3.2 20.2 %all-to-all-start.1 = ((bf16[4,8,1]{1,2,0:T(2,128)(2,1)}), bf16[4,8,1]{1,2,0:T(2,128)(2,1)S(1)}, u32[]{:S(2)}, u32[]{:S(2)}) async-start(bf16[4,8,1]{1,2,0:T(2,128)(2,1)} %reshape.598), calls=%async_computation.1 | async-start | bytes 4096 | tf_op jit(solution)/shard_map/all_to_all | solution.py:120
  11.1 102.1 %copy-start.29 = (pred[32]{0:T(512)(128)(4,1)}, pred[32]{0:T(512)(128)(4,1)S(1)}, u32[]{:S(2)}) copy-start(pred[32]{0:T(512)(128)(4,1)S(1)} %get-tuple-element.46) | copy-start | bytes 100
  23.4 10.7 %all-to-all-start.3 = ((bf16[4,8,4]{1,2,0:T(4,128)(2,1)}), bf16[4,8,4]{1,2,0:T(4,128)(2,1)S(1)}, u32[]{:S(2)}, u32[]{:S(2)}) async-start(bf16[4,8,4]{1,2,0:T(4,128)(2,1)} %copy.229), calls=%async_computation.3 | async-start | bytes 8192 | tf_op jit(solution)/shard_map/all_to_all | solution.py:170
  34.1 8.6 %all-to-all-start.6 = ((bf16[4,8,4]{1,2,0:T(4,128)(2,1)}), bf16[4,8,4]{1,2,0:T(4,128)(2,1)S(1)}, u32[]{:S(2)}, u32[]{:S(2)}) async-start(bf16[4,8,4]{1,2,0:T(4,128)(2,1)} %copy.235), calls=%async_computation.6 | async-start | bytes 8192 | tf_op jit(solution)/shard_map/all_to_all | solution.py:170
  42.7 8.8 %all-to-all-start.9 = ((bf16[4,8,4]{1,2,0:T(4,128)(2,1)}), bf16[4,8,4]{1,2,0:T(4,128)(2,1)S(1)}, u32[]{:S(2)}, u32[]{:S(2)}) async-start(bf16[4,8,4]{1,2,0:T(4,128)(2,1)} %copy.240), calls=%async_computation.9 | async-start | bytes 8192 | tf_op jit(solution)/shard_map/all_to_all | solution.py:170
  51.5 9.0 %all-to-all-start = ((bf16[4,8,1024]{2,1,0:T(8,128)(2,1)}), bf16[4,8,1024]{2,1,0:T(8,128)(2,1)S(1)}, u32[]{:S(2)}, u32[]{:S(2)}) async-start(bf16[4,8,1024]{2,1,0:T(8,128)(2,1)} %fusion.14), calls=%async_computation | async-start | bytes 131072 | tf_op jit(solution)/shard_map/all_to_all | solution.py:119
  60.5 16.7 %all-to-all-start.12 = ((bf16[4,8,4]{1,2,0:T(4,128)(2,1)}), bf16[4,8,4]{1,2,0:T(4,128)(2,1)S(1)}, u32[]{:S(2)}, u32[]{:S(2)}) async-start(bf16[4,8,4]{1,2,0:T(4,128)(2,1)} %copy.245), calls=%async_computation.12 | async-start | bytes 8192 | tf_op jit(solution)/shard_map/all_to_all | solution.py:170
  77.2 10.7 %all-to-all-start.2 = ((bf16[4,8,2048]{2,1,0:T(8,128)(2,1)}), bf16[4,8,2048]{2,1,0:T(8,128)(2,1)S(1)}, u32[]{:S(2)}, u32[]{:S(2)}) async-start(bf16[4,8,2048]{2,1,0:T(8,128)(2,1)} %fusion.52), calls=%async_computation.2 | async-start | bytes 262144 | tf_op jit(solution)/shard_map/all_to_all | solution.py:142
  89.4 9.7 %all-to-all-start.13 = ((bf16[4,8,1024]{2,1,0:T(8,128)(2,1)}), bf16[4,8,1024]{2,1,0:T(8,128)(2,1)S(1)}, u32[]{:S(2)}, u32[]{:S(2)}) async-start(bf16[4,8,1024]{2,1,0:T(8,128)(2,1)} %fusion.18), calls=%async_computation.13 | async-start | bytes 131072 | tf_op jit(solution)/shard_map/all_to_all | solution.py:169
  99.1 10.8 %all-to-all-start.10 = ((bf16[4,8,1024]{2,1,0:T(8,128)(2,1)}), bf16[4,8,1024]{2,1,0:T(8,128)(2,1)S(1)}, u32[]{:S(2)}, u32[]{:S(2)}) async-start(bf16[4,8,1024]{2,1,0:T(8,128)(2,1)} %fusion.17), calls=%async_computation.10 | async-start | bytes 131072 | tf_op jit(solution)/shard_map/all_to_all | solution.py:169
  109.9 9.0 %all-to-all-start.7 = ((bf16[4,8,1024]{2,1,0:T(8,128)(2,1)}), bf16[4,8,1024]{2,1,0:T(8,128)(2,1)S(1)}, u32[]{:S(2)}, u32[]{:S(2)}) async-start(bf16[4,8,1024]{2,1,0:T(8,128)(2,1)} %fusion.16), calls=%async_computation.7 | async-start | bytes 131072 | tf_op jit(solution)/shard_map/all_to_all | solution.py:169
  118.9 9.0 %all-to-all-start.4 = ((bf16[4,8,1024]{2,1,0:T(8,128)(2,1)}), bf16[4,8,1024]{2,1,0:T(8,128)(2,1)S(1)}, u32[]{:S(2)}, u32[]{:S(2)}) async-start(bf16[4,8,1024]{2,1,0:T(8,128)(2,1)} %fusion.15), calls=%async_computation.4 | async-start | bytes 131072 | tf_op jit(solution)/shard_map/all_to_all | solution.py:169
  127.9 10.0 %all-to-all-start.20 = ((f32[4,8,8]{1,2,0:T(8,128)}), f32[4,8,8]{1,2,0:T(8,128)S(1)}, u32[]{:S(2)}, u32[]{:S(2)}) async-start(f32[4,8,8]{1,2,0:T(8,128)} %copy.265), calls=%async_computation.20 | async-start | bytes 32768 | tf_op jit(solution)/shard_map/all_to_all | solution.py:177
  137.9 8.8 %all-to-all-start.8 = ((f32[4,8,8]{1,2,0:T(8,128)}), f32[4,8,8]{1,2,0:T(8,128)S(1)}, u32[]{:S(2)}, u32[]{:S(2)}) async-start(f32[4,8,8]{1,2,0:T(8,128)} %copy.238), calls=%async_computation.8 | async-start | bytes 32768 | tf_op jit(solution)/shard_map/all_to_all | solution.py:176
  146.7 8.8 %all-to-all-start.21 = ((f32[4,8,8]{1,2,0:T(8,128)}), f32[4,8,8]{1,2,0:T(8,128)S(1)}, u32[]{:S(2)}, u32[]{:S(2)}) async-start(f32[4,8,8]{1,2,0:T(8,128)} %copy.267), calls=%async_computation.21 | async-start | bytes 32768 | tf_op jit(solution)/shard_map/all_to_all | solution.py:177
  155.5 8.8 %all-to-all-start.11 = ((f32[4,8,8]{1,2,0:T(8,128)}), f32[4,8,8]{1,2,0:T(8,128)S(1)}, u32[]{:S(2)}, u32[]{:S(2)}) async-start(f32[4,8,8]{1,2,0:T(8,128)} %copy.243), calls=%async_computation.11 | async-start | bytes 32768 | tf_op jit(solution)/shard_map/all_to_all | solution.py:176
  164.4 8.8 %all-to-all-start.22 = ((f32[4,8,8]{1,2,0:T(8,128)}), f32[4,8,8]{1,2,0:T(8,128)S(1)}, u32[]{:S(2)}, u32[]{:S(2)}) async-start(f32[4,8,8]{1,2,0:T(8,128)} %copy.269), calls=%async_computation.22 | async-start | bytes 32768 | tf_op jit(solution)/shard_map/all_to_all | solution.py:177
  173.2 8.8 %all-to-all-start.14 = ((f32[4,8,8]{1,2,0:T(8,128)}), f32[4,8,8]{1,2,0:T(8,128)S(1)}, u32[]{:S(2)}, u32[]{:S(2)}) async-start(f32[4,8,8]{1,2,0:T(8,128)} %copy.248), calls=%async_computation.14 | async-start | bytes 32768 | tf_op jit(solution)/shard_map/all_to_all | solution.py:176
  182.0 9.3 %all-to-all-start.19 = ((f32[4,8,8]{1,2,0:T(8,128)}), f32[4,8,8]{1,2,0:T(8,128)S(1)}, u32[]{:S(2)}, u32[]{:S(2)}) async-start(f32[4,8,8]{1,2,0:T(8,128)} %copy.263), calls=%async_computation.19 | async-start | bytes 32768 | tf_op jit(solution)/shard_map/all_to_all | solution.py:177
  191.4 8.8 %all-to-all-start.5 = ((f32[4,8,8]{1,2,0:T(8,128)}), f32[4,8,8]{1,2,0:T(8,128)S(1)}, u32[]{:S(2)}, u32[]{:S(2)}) async-start(f32[4,8,8]{1,2,0:T(8,128)} %copy.233), calls=%async_computation.5 | async-start | bytes 32768 | tf_op jit(solution)/shard_map/all_to_all | solution.py:176
  200.2 9.2 %all-to-all-start.16 = ((f32[4,8,1024]{2,1,0:T(8,128)}), f32[4,8,1024]{2,1,0:T(8,128)S(1)}, u32[]{:S(2)}, u32[]{:S(2)}) async-start(f32[4,8,1024]{2,1,0:T(8,128)} %bitcast.311), calls=%async_computation.16 | async-start | bytes 262144 | tf_op jit(solution)/shard_map/all_to_all | solution.py:175
  209.4 9.6 %all-to-all-start.17 = ((f32[4,8,1024]{2,1,0:T(8,128)}), f32[4,8,1024]{2,1,0:T(8,128)S(1)}, u32[]{:S(2)}, u32[]{:S(2)}) async-start(f32[4,8,1024]{2,1,0:T(8,128)} %bitcast.310), calls=%async_computation.17 | async-start | bytes 262144 | tf_op jit(solution)/shard_map/all_to_all | solution.py:175
  219.0 9.5 %all-to-all-start.18 = ((f32[4,8,1024]{2,1,0:T(8,128)}), f32[4,8,1024]{2,1,0:T(8,128)S(1)}, u32[]{:S(2)}, u32[]{:S(2)}) async-start(f32[4,8,1024]{2,1,0:T(8,128)} %bitcast.309), calls=%async_computation.18 | async-start | bytes 262144 | tf_op jit(solution)/shard_map/all_to_all | solution.py:175
  228.5 9.2 %all-to-all-start.15 = ((f32[4,8,1024]{2,1,0:T(8,128)}), f32[4,8,1024]{2,1,0:T(8,128)S(1)}, u32[]{:S(2)}, u32[]{:S(2)}) async-start(f32[4,8,1024]{2,1,0:T(8,128)} %bitcast.312), calls=%async_computation.15 | async-start | bytes 262144 | tf_op jit(solution)/shard_map/all_to_all | solution.py:175
  (40 other events, 1577.7 us)
where the time goes:
time: 241 us; the launch traced here: 239 us
  waiting for transfers between devices  88.2 us (37%)
  starting transfers between devices  85.2 us (35%)
  matrix products  21.9 us (9%)
  local copies, waits for them, and re-layouts  18 us (7%)
  other arithmetic  12.8 us (5%)
  blocking collectives  10.4 us (4%)
    all_to_all x4, waiting for transfers between devices, body(): lax.all_to_all(answer_mixed_rows, 'hosts', split_axis=0, concat_axis=0, t...  21.8 us
    all_to_all x4, waiting for transfers between devices, body(): lax.all_to_all(answer_totals, 'hosts', split_axis=0, concat_axis=0, tiled...  16.1 us
    all_to_all x4, waiting for transfers between devices, body(): lax.all_to_all(request[3], 'hosts', split_axis=0, concat_axis=0, tiled=True)  15.3 us
    all_to_all x4, starting transfers between devices, body(): lax.all_to_all(request[2], 'hosts', split_axis=0, concat_axis=0, tiled=True)  14.9 us
    all_to_all x4, starting transfers between devices, body(): lax.all_to_all(request[3], 'hosts', split_axis=0, concat_axis=0, tiled=True)  14.8 us
    all_to_all x4, starting transfers between devices, body(): lax.all_to_all(answer_totals, 'hosts', split_axis=0, concat_axis=0, tiled...  14.5 us
    all_to_all x4, waiting for transfers between devices, body(): lax.all_to_all(answer_top_score, 'hosts', split_axis=0, concat_axis=0, ti...  14.2 us
    all_to_all x4, starting transfers between devices, body(): lax.all_to_all(answer_mixed_rows, 'hosts', split_axis=0, concat_axis=0, t...  13.5 us
  transfers between devices with their start and end apart: 23, of which 20 were waited for; matrix products, arithmetic and copies ran while one was open for 20% of the time, Pallas kernels for 0%

commit v1 on v0

--- a/solution.py
+++ b/solution.py
@@ -10,6 +10,26 @@
 ADAPTER_SCALE = 0.5
 ROPE_BASE = 10000.0
 NEG_FILL = -1e30
+
+
+def wait_set_over_axis(out_dim, mine_x, axis_k):
+    local_next = lax.axis_size("hosts")
+    g_now = lax.axis_index("hosts")
+    current_value, r2 = (local_next, g_now)
+    top = mine_x.shape[axis_k] // current_value
+    x_new = list(mine_x.shape)
+    x_new[axis_k] = top
+    arr_out = x_new[out_dim]
+    x_new[out_dim] = arr_out * current_value
+    k_now = jnp.zeros(x_new, mine_x.dtype)
+    for q in tuple(range(current_value)):
+        mixed_arr = lax.dynamic_slice_in_dim(mine_x, (r2 ^ q) * top, top, axis=axis_k)
+        if q:
+            mixed_arr = lax.ppermute(
+                mixed_arr, "hosts", [(no, no ^ q) for no in range(current_value)]
+            )
+        k_now = lax.dynamic_update_slice_in_dim(k_now, mixed_arr, (r2 ^ q) * arr_out, axis=out_dim)
+    return k_now
 
 
 def rotate(values, position):
@@ -174,7 +194,7 @@
             (
                 lax.all_to_all(answer_mixed_rows, "hosts", split_axis=0, concat_axis=0, tiled=True),
                 lax.all_to_all(answer_top_score, "hosts", split_axis=0, concat_axis=0, tiled=True),
-                lax.all_to_all(answer_totals, "hosts", split_axis=0, concat_axis=0, tiled=True),
+                wait_set_over_axis(0, answer_totals, 0),
             )
         )
     entries = []

time: 241 us -> 221 us (0.917)
  waiting for transfers between devices: 88.2 us -> 75.9 us
  starting transfers between devices: 85.2 us -> 92.3 us
  matrix products: 21.9 us -> 15 us
  other arithmetic: 12.8 us -> 7.94 us
    ppermute x0 -> x12, starting transfers between devices: none -> 18.7 us  [wait_set_over_axis(): lax.ppermute(mixed_arr, 'hosts', [(no, no ^ q) for no in range(current_va...]
    all_to_all x4 -> x0, waiting for transfers between devices: 16.1 us -> none  [body(): lax.all_to_all(answer_totals, 'hosts', split_axis=0, concat_axis=0, tiled...]
    all_to_all x4 -> x0, starting transfers between devices: 14.5 us -> none  [body(): lax.all_to_all(answer_totals, 'hosts', split_axis=0, concat_axis=0, tiled...]
    all_to_all x4, starting transfers between devices: 13 us -> 17.8 us  [body(): lax.all_to_all(answer_top_score, 'hosts', split_axis=0, concat_axis=0, ti...]
    all_to_all x4, waiting for transfers between devices: 14.2 us -> 10.6 us  [body(): lax.all_to_all(answer_top_score, 'hosts', split_axis=0, concat_axis=0, ti...]
    all_to_all x4, waiting for transfers between devices: 10.3 us -> 13.8 us  [body(): lax.all_to_all(request[2], 'hosts', split_axis=0, concat_axis=0, tiled=True)]
    dot_general x4, matrix products: 4.56 us -> 1.89 us  [attend_local(): jnp.einsum('ncbht,bthd->nchd', weights.astype(jnp.bfloat16), block_values...]
    reduce_sum x4 -> x0, local copies, waits for them, and re-layouts: 2.43 us -> none  [attend_local(): totals = jnp.sum(weights, axis=(2, 4))]
  transfers between devices with their start and end apart: 23 -> 31, of which waited for: 20 -> 16; matrix products, arithmetic and copies ran while one was open for 20% -> 14% of each run, Pallas kernels for 0% -> 0%
where the time goes in v1:
time: 221 us; the launch traced here: 220 us
  starting transfers between devices  92.3 us (42%)
  waiting for transfers between devices  75.9 us (34%)
  local copies, waits for them, and re-layouts  16 us (7%)
  matrix products  15 us (7%)
  blocking collectives  10.4 us (5%)
  other arithmetic  7.94 us (4%)
    all_to_all x4, waiting for transfers between devices, body(): lax.all_to_all(answer_mixed_rows, 'hosts', split_axis=0, concat_axis=0, t...  22 us
    ppermute x12, starting transfers between devices, wait_set_over_axis(): lax.ppermute(mixed_arr, 'hosts', [(no, no ^ q) for no in range(current_va...  18.7 us
    all_to_all x4, starting transfers between devices, body(): lax.all_to_all(answer_top_score, 'hosts', split_axis=0, concat_axis=0, ti...  17.8 us
    all_to_all x4, waiting for transfers between devices, body(): lax.all_to_all(request[3], 'hosts', split_axis=0, concat_axis=0, tiled=True)  16.5 us
    all_to_all x4, starting transfers between devices, body(): lax.all_to_all(request[3], 'hosts', split_axis=0, concat_axis=0, tiled=True)  14.9 us
    all_to_all x4, waiting for transfers between devices, body(): lax.all_to_all(request[2], 'hosts', split_axis=0, concat_axis=0, tiled=True)  13.8 us
    all_to_all x4, starting transfers between devices, body(): lax.all_to_all(answer_mixed_rows, 'hosts', split_axis=0, concat_axis=0, t...  13.3 us
    all_to_all x4, starting transfers between devices, body(): lax.all_to_all(request[2], 'hosts', split_axis=0, concat_axis=0, tiled=True)  13.1 us
  transfers between devices with their start and end apart: 31, of which 16 were waited for; matrix products, arithmetic and copies ran while one was open for 14% of the time, Pallas kernels for 0%

profile of v1, /device:TPU:0, one launch (start us, length us, event | category | flops | bytes accessed | tf_op | source)
XLA Modules:
  0.0 219.6 jit_solution(1898454604206502019)
XLA Ops:
  3.1 6.3 %all-to-all-start.1 = ((bf16[4,8,1]{1,2,0:T(2,128)(2,1)}), bf16[4,8,1]{1,2,0:T(2,128)(2,1)S(1)}, u32[]{:S(2)}, u32[]{:S(2)}) async-start(bf16[4,8,1]{1,2,0:T(2,128)(2,1)} %reshape.598), calls=%async_computation.1 | async-start | bytes 4096 | tf_op jit(solution)/shard_map/all_to_all | solution.py:140
  24.1 5.2 %all-to-all-start.3 = ((bf16[4,8,4]{1,2,0:T(4,128)(2,1)}), bf16[4,8,4]{1,2,0:T(4,128)(2,1)S(1)}, u32[]{:S(2)}, u32[]{:S(2)}) async-start(bf16[4,8,4]{1,2,0:T(4,128)(2,1)} %copy.178), calls=%async_computation.3 | async-start | bytes 8192 | tf_op jit(solution)/shard_map/all_to_all | solution.py:190
  29.3 5.6 %all-to-all-done.3 = bf16[4,8,4]{1,2,0:T(4,128)(2,1)S(1)} async-done(((bf16[4,8,4]{1,2,0:T(4,128)(2,1)}), bf16[4,8,4]{1,2,0:T(4,128)(2,1)S(1)}, u32[]{:S(2)}, u32[]{:S(2)}) %all-to-all-start.3) | async-done | bytes 288 | tf_op jit(solution)/shard_map/all_to_all | solution.py:190
  38.1 5.4 %all-to-all-done.6 = bf16[4,8,4]{1,2,0:T(4,128)(2,1)S(1)} async-done(((bf16[4,8,4]{1,2,0:T(4,128)(2,1)}), bf16[4,8,4]{1,2,0:T(4,128)(2,1)S(1)}, u32[]{:S(2)}, u32[]{:S(2)}) %all-to-all-start.6) | async-done | bytes 288 | tf_op jit(solution)/shard_map/all_to_all | solution.py:190
  46.8 5.5 %all-to-all-done.9 = bf16[4,8,4]{1,2,0:T(4,128)(2,1)S(1)} async-done(((bf16[4,8,4]{1,2,0:T(4,128)(2,1)}), bf16[4,8,4]{1,2,0:T(4,128)(2,1)S(1)}, u32[]{:S(2)}, u32[]{:S(2)}) %all-to-all-start.9) | async-done | bytes 288 | tf_op jit(solution)/shard_map/all_to_all | solution.py:190
  55.6 5.7 %all-to-all-done = bf16[4,8,1024]{2,1,0:T(8,128)(2,1)S(1)} async-done(((bf16[4,8,1024]{2,1,0:T(8,128)(2,1)}), bf16[4,8,1024]{2,1,0:T(8,128)(2,1)S(1)}, u32[]{:S(2)}, u32[]{:S(2)}) %all-to-all-start) | async-done | bytes 65568 | tf_op jit(solution)/shard_map/all_to_all | solution.py:139
  64.7 10.4 %psum.7 = bf16[4,8,128]{2,1,0:T(8,128)(2,1)S(1)} all-reduce(f32[4,8,128]{2,1,0:T(8,128)S(1)} %convolution_multiply_fusion.8), channel_id=1, replica_groups=mesh['groups'=2,'hosts'=4,'mp'=4] {'mp'}, use_global_device_ids=true, to_apply=%region_2.3 | all-reduce | flops 4096 | bytes 24576 | tf_op jit(solution)/shard_map/psum | solution.py:145
  76.3 4.8 %all-to-all-start.2 = ((bf16[4,8,2048]{2,1,0:T(8,128)(2,1)}), bf16[4,8,2048]{2,1,0:T(8,128)(2,1)S(1)}, u32[]{:S(2)}, u32[]{:S(2)}) async-start(bf16[4,8,2048]{2,1,0:T(8,128)(2,1)} %fusion.52), calls=%async_computation.2 | async-start | bytes 262144 | tf_op jit(solution)/shard_map/all_to_all | solution.py:162
  81.0 5.9 %all-to-all-done.2 = bf16[4,8,2048]{2,1,0:T(8,128)(2,1)S(1)} async-done(((bf16[4,8,2048]{2,1,0:T(8,128)(2,1)}), bf16[4,8,2048]{2,1,0:T(8,128)(2,1)S(1)}, u32[]{:S(2)}, u32[]{:S(2)}) %all-to-all-start.2) | async-done | bytes 131104 | tf_op jit(solution)/shard_map/all_to_all | solution.py:162
  104.4 4.0 %all-to-all-done.7 = bf16[4,8,1024]{2,1,0:T(8,128)(2,1)S(1)} async-done(((bf16[4,8,1024]{2,1,0:T(8,128)(2,1)}), bf16[4,8,1024]{2,1,0:T(8,128)(2,1)S(1)}, u32[]{:S(2)}, u32[]{:S(2)}) %all-to-all-start.7) | async-done | bytes 65568 | tf_op jit(solution)/shard_map/all_to_all | solution.py:189
  113.3 4.0 %all-to-all-done.10 = bf16[4,8,1024]{2,1,0:T(8,128)(2,1)S(1)} async-done(((bf16[4,8,1024]{2,1,0:T(8,128)(2,1)}), bf16[4,8,1024]{2,1,0:T(8,128)(2,1)S(1)}, u32[]{:S(2)}, u32[]{:S(2)}) %all-to-all-start.10) | async-done | bytes 65568 | tf_op jit(solution)/shard_map/all_to_all | solution.py:189
  122.3 4.0 %all-to-all-done.13 = bf16[4,8,1024]{2,1,0:T(8,128)(2,1)S(1)} async-done(((bf16[4,8,1024]{2,1,0:T(8,128)(2,1)}), bf16[4,8,1024]{2,1,0:T(8,128)(2,1)S(1)}, u32[]{:S(2)}, u32[]{:S(2)}) %all-to-all-start.13) | async-done | bytes 65568 | tf_op jit(solution)/shard_map/all_to_all | solution.py:189
  134.6 4.4 %all-to-all-start.11 = ((f32[4,8,8]{1,2,0:T(8,128)}), f32[4,8,8]{1,2,0:T(8,128)S(1)}, u32[]{:S(2)}, u32[]{:S(2)}) async-start(f32[4,8,8]{1,2,0:T(8,128)} %copy.192), calls=%async_computation.11 | async-start | bytes 32768 | tf_op jit(solution)/shard_map/all_to_all | solution.py:196
  141.2 3.9 %collective-permute-start.5 = (f32[1,8,8]{1,0,2:T(1,128)S(1)}, f32[1,8,8]{1,0,2:T(1,128)S(1)}, u32[]{:S(2)}, u32[]{:S(2)}) collective-permute-start(f32[1,8,8]{1,0,2:T(1,128)S(1)} %get-tuple-element.33), channel_id=1, source_target_pairs={{0,12},{4,8},{8,4},{12,0},{1,13},{5,9},{9,5},{13,1},{2,14},{6,10},... | collective-permute-start | bytes 776 | tf_op jit(solution)/shard_map/ppermute | solution.py:28
  146.0 5.1 %all-to-all-start.8 = ((f32[4,8,8]{1,2,0:T(8,128)}), f32[4,8,8]{1,2,0:T(8,128)S(1)}, u32[]{:S(2)}, u32[]{:S(2)}) async-start(f32[4,8,8]{1,2,0:T(8,128)} %copy.187), calls=%async_computation.8 | async-start | bytes 32768 | tf_op jit(solution)/shard_map/all_to_all | solution.py:196
  151.1 3.8 %collective-permute-start.8 = (f32[1,8,8]{1,0,2:T(1,128)S(1)}, f32[1,8,8]{1,0,2:T(1,128)S(1)}, u32[]{:S(2)}, u32[]{:S(2)}) collective-permute-start(f32[1,8,8]{1,0,2:T(1,128)S(1)} %get-tuple-element.37), channel_id=1, source_target_pairs={{0,12},{4,8},{8,4},{12,0},{1,13},{5,9},{9,5},{13,1},{2,14},{6,10},... | collective-permute-start | bytes 776 | tf_op jit(solution)/shard_map/ppermute | solution.py:28
  155.9 3.8 %collective-permute-start.11 = (f32[1,8,8]{1,0,2:T(1,128)S(1)}, f32[1,8,8]{1,0,2:T(1,128)S(1)}, u32[]{:S(2)}, u32[]{:S(2)}) collective-permute-start(f32[1,8,8]{1,0,2:T(1,128)S(1)} %get-tuple-element.41), channel_id=1, source_target_pairs={{0,12},{4,8},{8,4},{12,0},{1,13},{5,9},{9,5},{13,1},{2,14},{6,10},... | collective-permute-start | bytes 776 | tf_op jit(solution)/shard_map/ppermute | solution.py:28
  161.5 5.1 %all-to-all-start.14 = ((f32[4,8,8]{1,2,0:T(8,128)}), f32[4,8,8]{1,2,0:T(8,128)S(1)}, u32[]{:S(2)}, u32[]{:S(2)}) async-start(f32[4,8,8]{1,2,0:T(8,128)} %copy.197), calls=%async_computation.14 | async-start | bytes 32768 | tf_op jit(solution)/shard_map/all_to_all | solution.py:196
  166.9 5.3 %all-to-all-done.14 = f32[4,8,8]{1,2,0:T(8,128)S(1)} async-done(((f32[4,8,8]{1,2,0:T(8,128)}), f32[4,8,8]{1,2,0:T(8,128)S(1)}, u32[]{:S(2)}, u32[]{:S(2)}) %all-to-all-start.14) | async-done | bytes 1056 | tf_op jit(solution)/shard_map/all_to_all | solution.py:196
  175.7 5.3 %all-to-all-done.5 = f32[4,8,8]{1,2,0:T(8,128)S(1)} async-done(((f32[4,8,8]{1,2,0:T(8,128)}), f32[4,8,8]{1,2,0:T(8,128)S(1)}, u32[]{:S(2)}, u32[]{:S(2)}) %all-to-all-start.5) | async-done | bytes 1056 | tf_op jit(solution)/shard_map/all_to_all | solution.py:196
  185.7 4.5 %all-to-all-done.16 = f32[4,8,1024]{2,1,0:T(8,128)S(1)} async-done(((f32[4,8,1024]{2,1,0:T(8,128)}), f32[4,8,1024]{2,1,0:T(8,128)S(1)}, u32[]{:S(2)}, u32[]{:S(2)}) %all-to-all-start.16) | async-done | bytes 131104 | tf_op jit(solution)/shard_map/all_to_all | solution.py:195
  193.9 6.2 %all-to-all-done.17 = f32[4,8,1024]{2,1,0:T(8,128)S(1)} async-done(((f32[4,8,1024]{2,1,0:T(8,128)}), f32[4,8,1024]{2,1,0:T(8,128)S(1)}, u32[]{:S(2)}, u32[]{:S(2)}) %all-to-all-start.17) | async-done | bytes 131104 | tf_op jit(solution)/shard_map/all_to_all | solution.py:195
  203.7 5.7 %all-to-all-done.18 = f32[4,8,1024]{2,1,0:T(8,128)S(1)} async-done(((f32[4,8,1024]{2,1,0:T(8,128)}), f32[4,8,1024]{2,1,0:T(8,128)S(1)}, u32[]{:S(2)}, u32[]{:S(2)}) %all-to-all-start.18) | async-done | bytes 131104 | tf_op jit(solution)/shard_map/all_to_all | solution.py:195
  213.0 5.6 %all-to-all-done.15 = f32[4,8,1024]{2,1,0:T(8,128)S(1)} async-done(((f32[4,8,1024]{2,1,0:T(8,128)}), f32[4,8,1024]{2,1,0:T(8,128)S(1)}, u32[]{:S(2)}, u32[]{:S(2)}) %all-to-all-start.15) | async-done | bytes 131104 | tf_op jit(solution)/shard_map/all_to_all | solution.py:195
  (215 shorter events, 92.1 us)
Async XLA Ops:
  3.1 21.0 %all-to-all-start.1 = ((bf16[4,8,1]{1,2,0:T(2,128)(2,1)}), bf16[4,8,1]{1,2,0:T(2,128)(2,1)S(1)}, u32[]{:S(2)}, u32[]{:S(2)}) async-start(bf16[4,8,1]{1,2,0:T(2,128)(2,1)} %reshape.598), calls=%async_computation.1 | async-start | bytes 4096 | tf_op jit(solution)/shard_map/all_to_all | solution.py:140
  24.1 10.8 %all-to-all-start.3 = ((bf16[4,8,4]{1,2,0:T(4,128)(2,1)}), bf16[4,8,4]{1,2,0:T(4,128)(2,1)S(1)}, u32[]{:S(2)}, u32[]{:S(2)}) async-start(bf16[4,8,4]{1,2,0:T(4,128)(2,1)} %copy.178), calls=%async_computation.3 | async-start | bytes 8192 | tf_op jit(solution)/shard_map/all_to_all | solution.py:190
  52.3 9.0 %all-to-all-start = ((bf16[4,8,1024]{2,1,0:T(8,128)(2,1)}), bf16[4,8,1024]{2,1,0:T(8,128)(2,1)S(1)}, u32[]{:S(2)}, u32[]{:S(2)}) async-start(bf16[4,8,1024]{2,1,0:T(8,128)(2,1)} %fusion.14), calls=%async_computation | async-start | bytes 131072 | tf_op jit(solution)/shard_map/all_to_all | solution.py:139
  61.3 14.9 %all-to-all-start.12 = ((bf16[4,8,4]{1,2,0:T(4,128)(2,1)}), bf16[4,8,4]{1,2,0:T(4,128)(2,1)S(1)}, u32[]{:S(2)}, u32[]{:S(2)}) async-start(bf16[4,8,4]{1,2,0:T(4,128)(2,1)} %copy.194), calls=%async_computation.12 | async-start | bytes 8192 | tf_op jit(solution)/shard_map/all_to_all | solution.py:190
  76.3 10.7 %all-to-all-start.2 = ((bf16[4,8,2048]{2,1,0:T(8,128)(2,1)}), bf16[4,8,2048]{2,1,0:T(8,128)(2,1)S(1)}, u32[]{:S(2)}, u32[]{:S(2)}) async-start(bf16[4,8,2048]{2,1,0:T(8,128)(2,1)} %fusion.52), calls=%async_computation.2 | async-start | bytes 262144 | tf_op jit(solution)/shard_map/all_to_all | solution.py:162
  90.3 9.0 %all-to-all-start.4 = ((bf16[4,8,1024]{2,1,0:T(8,128)(2,1)}), bf16[4,8,1024]{2,1,0:T(8,128)(2,1)S(1)}, u32[]{:S(2)}, u32[]{:S(2)}) async-start(bf16[4,8,1024]{2,1,0:T(8,128)(2,1)} %fusion.15), calls=%async_computation.4 | async-start | bytes 131072 | tf_op jit(solution)/shard_map/all_to_all | solution.py:189
  99.3 9.0 %all-to-all-start.7 = ((bf16[4,8,1024]{2,1,0:T(8,128)(2,1)}), bf16[4,8,1024]{2,1,0:T(8,128)(2,1)S(1)}, u32[]{:S(2)}, u32[]{:S(2)}) async-start(bf16[4,8,1024]{2,1,0:T(8,128)(2,1)} %fusion.16), calls=%async_computation.7 | async-start | bytes 131072 | tf_op jit(solution)/shard_map/all_to_all | solution.py:189
  108.3 9.0 %all-to-all-start.10 = ((bf16[4,8,1024]{2,1,0:T(8,128)(2,1)}), bf16[4,8,1024]{2,1,0:T(8,128)(2,1)S(1)}, u32[]{:S(2)}, u32[]{:S(2)}) async-start(bf16[4,8,1024]{2,1,0:T(8,128)(2,1)} %fusion.17), calls=%async_computation.10 | async-start | bytes 131072 | tf_op jit(solution)/shard_map/all_to_all | solution.py:189
  117.3 9.0 %all-to-all-start.13 = ((bf16[4,8,1024]{2,1,0:T(8,128)(2,1)}), bf16[4,8,1024]{2,1,0:T(8,128)(2,1)S(1)}, u32[]{:S(2)}, u32[]{:S(2)}) async-start(bf16[4,8,1024]{2,1,0:T(8,128)(2,1)} %fusion.18), calls=%async_computation.13 | async-start | bytes 131072 | tf_op jit(solution)/shard_map/all_to_all | solution.py:189
  128.7 12.5 %collective-permute-start = (f32[1,8,8]{1,0,2:T(1,128)S(1)}, f32[1,8,8]{1,0,2:T(1,128)S(1)}, u32[]{:S(2)}, u32[]{:S(2)}) collective-permute-start(f32[1,8,8]{1,0,2:T(1,128)S(1)} %get-tuple-element.31), channel_id=1, source_target_pairs={{0,4},{4,0},{8,12},{12,8},{1,5},{5,1},{9,13},{13,9},{2,6},{6,2},{1... | collective-permute-start | bytes 776 | tf_op jit(solution)/shard_map/ppermute | solution.py:28
  129.7 15.4 %collective-permute-start.1 = (f32[1,8,8]{1,0,2:T(1,128)S(1)}, f32[1,8,8]{1,0,2:T(1,128)S(1)}, u32[]{:S(2)}, u32[]{:S(2)}) collective-permute-start(f32[1,8,8]{1,0,2:T(1,128)S(1)} %get-tuple-element.30), channel_id=1, source_target_pairs={{0,8},{4,12},{8,0},{12,4},{1,9},{5,13},{9,1},{13,5},{2,10},{6,14},... | collective-permute-start | bytes 776 | tf_op jit(solution)/shard_map/ppermute | solution.py:28
  130.1 15.2 %collective-permute-start.2 = (f32[1,8,8]{1,0,2:T(1,128)S(1)}, f32[1,8,8]{1,0,2:T(1,128)S(1)}, u32[]{:S(2)}, u32[]{:S(2)}) collective-permute-start(f32[1,8,8]{1,0,2:T(1,128)S(1)} %get-tuple-element.29), channel_id=1, source_target_pairs={{0,12},{4,8},{8,4},{12,0},{1,13},{5,9},{9,5},{13,1},{2,14},{6,10},... | collective-permute-start | bytes 776 | tf_op jit(solution)/shard_map/ppermute | solution.py:28
  133.2 17.9 %collective-permute-start.3 = (f32[1,8,8]{1,0,2:T(1,128)S(1)}, f32[1,8,8]{1,0,2:T(1,128)S(1)}, u32[]{:S(2)}, u32[]{:S(2)}) collective-permute-start(f32[1,8,8]{1,0,2:T(1,128)S(1)} %get-tuple-element.35), channel_id=1, source_target_pairs={{0,4},{4,0},{8,12},{12,8},{1,5},{5,1},{9,13},{13,9},{2,6},{6,2},{1... | collective-permute-start | bytes 776 | tf_op jit(solution)/shard_map/ppermute | solution.py:28
  133.3 21.7 %collective-permute-start.4 = (f32[1,8,8]{1,0,2:T(1,128)S(1)}, f32[1,8,8]{1,0,2:T(1,128)S(1)}, u32[]{:S(2)}, u32[]{:S(2)}) collective-permute-start(f32[1,8,8]{1,0,2:T(1,128)S(1)} %get-tuple-element.34), channel_id=1, source_target_pairs={{0,8},{4,12},{8,0},{12,4},{1,9},{5,13},{9,1},{13,5},{2,10},{6,14},... | collective-permute-start | bytes 776 | tf_op jit(solution)/shard_map/ppermute | solution.py:28
  134.6 11.5 %all-to-all-start.11 = ((f32[4,8,8]{1,2,0:T(8,128)}), f32[4,8,8]{1,2,0:T(8,128)S(1)}, u32[]{:S(2)}, u32[]{:S(2)}) async-start(f32[4,8,8]{1,2,0:T(8,128)} %copy.192), calls=%async_computation.11 | async-start | bytes 32768 | tf_op jit(solution)/shard_map/all_to_all | solution.py:196
  141.2 13.9 %collective-permute-start.5 = (f32[1,8,8]{1,0,2:T(1,128)S(1)}, f32[1,8,8]{1,0,2:T(1,128)S(1)}, u32[]{:S(2)}, u32[]{:S(2)}) collective-permute-start(f32[1,8,8]{1,0,2:T(1,128)S(1)} %get-tuple-element.33), channel_id=1, source_target_pairs={{0,12},{4,8},{8,4},{12,0},{1,13},{5,9},{9,5},{13,1},{2,14},{6,10},... | collective-permute-start | bytes 776 | tf_op jit(solution)/shard_map/ppermute | solution.py:28
  145.2 10.7 %collective-permute-start.6 = (f32[1,8,8]{1,0,2:T(1,128)S(1)}, f32[1,8,8]{1,0,2:T(1,128)S(1)}, u32[]{:S(2)}, u32[]{:S(2)}) collective-permute-start(f32[1,8,8]{1,0,2:T(1,128)S(1)} %get-tuple-element.39), channel_id=1, source_target_pairs={{0,4},{4,0},{8,12},{12,8},{1,5},{5,1},{9,13},{13,9},{2,6},{6,2},{1... | collective-permute-start | bytes 776 | tf_op jit(solution)/shard_map/ppermute | solution.py:28
  145.3 14.4 %collective-permute-start.7 = (f32[1,8,8]{1,0,2:T(1,128)S(1)}, f32[1,8,8]{1,0,2:T(1,128)S(1)}, u32[]{:S(2)}, u32[]{:S(2)}) collective-permute-start(f32[1,8,8]{1,0,2:T(1,128)S(1)} %get-tuple-element.38), channel_id=1, source_target_pairs={{0,8},{4,12},{8,0},{12,4},{1,9},{5,13},{9,1},{13,5},{2,10},{6,14},... | collective-permute-start | bytes 776 | tf_op jit(solution)/shard_map/ppermute | solution.py:28
  146.0 15.5 %all-to-all-start.8 = ((f32[4,8,8]{1,2,0:T(8,128)}), f32[4,8,8]{1,2,0:T(8,128)S(1)}, u32[]{:S(2)}, u32[]{:S(2)}) async-start(f32[4,8,8]{1,2,0:T(8,128)} %copy.187), calls=%async_computation.8 | async-start | bytes 32768 | tf_op jit(solution)/shard_map/all_to_all | solution.py:196
  161.5 10.7 %all-to-all-start.14 = ((f32[4,8,8]{1,2,0:T(8,128)}), f32[4,8,8]{1,2,0:T(8,128)S(1)}, u32[]{:S(2)}, u32[]{:S(2)}) async-start(f32[4,8,8]{1,2,0:T(8,128)} %copy.197), calls=%async_computation.14 | async-start | bytes 32768 | tf_op jit(solution)/shard_map/all_to_all | solution.py:196
  181.0 9.2 %all-to-all-start.16 = ((f32[4,8,1024]{2,1,0:T(8,128)}), f32[4,8,1024]{2,1,0:T(8,128)S(1)}, u32[]{:S(2)}, u32[]{:S(2)}) async-start(f32[4,8,1024]{2,1,0:T(8,128)} %bitcast.311), calls=%async_computation.16 | async-start | bytes 262144 | tf_op jit(solution)/shard_map/all_to_all | solution.py:195
  190.3 9.8 %all-to-all-start.17 = ((f32[4,8,1024]{2,1,0:T(8,128)}), f32[4,8,1024]{2,1,0:T(8,128)S(1)}, u32[]{:S(2)}, u32[]{:S(2)}) async-start(f32[4,8,1024]{2,1,0:T(8,128)} %bitcast.310), calls=%async_computation.17 | async-start | bytes 262144 | tf_op jit(solution)/shard_map/all_to_all | solution.py:195
  200.1 9.3 %all-to-all-start.18 = ((f32[4,8,1024]{2,1,0:T(8,128)}), f32[4,8,1024]{2,1,0:T(8,128)S(1)}, u32[]{:S(2)}, u32[]{:S(2)}) async-start(f32[4,8,1024]{2,1,0:T(8,128)} %bitcast.309), calls=%async_computation.18 | async-start | bytes 262144 | tf_op jit(solution)/shard_map/all_to_all | solution.py:195
  209.4 9.2 %all-to-all-start.15 = ((f32[4,8,1024]{2,1,0:T(8,128)}), f32[4,8,1024]{2,1,0:T(8,128)S(1)}, u32[]{:S(2)}, u32[]{:S(2)}) async-start(f32[4,8,1024]{2,1,0:T(8,128)} %bitcast.312), calls=%async_computation.15 | async-start | bytes 262144 | tf_op jit(solution)/shard_map/all_to_all | solution.py:195
  (21 other events, 489.6 us)
